TPU v7x, 32 devices: a whole 2x2x4 slice. The times are simulated.
32 devices in a mesh: dp: 8 (over y, x, core), mp: 4 (over z).
Axes of the slice: x: 2, y: 2, z: 4, core: 2. Of those that a mesh axis runs over, the one named last changes fastest.
Arguments:
- tokens: bfloat16 [16, 512, 768], P('dp'), may hold values from -6 to 6
- lengths: int32 [16], P('dp'), may hold values from 40 to 512, as said below
- coords: int32 [16, 2, 512], P('dp'), may hold values from 0 to 999
- w_qkv: bfloat16 [3, 768, 768], P(None, None, 'mp'), may hold values from -0.375 to 0.375
- w_pos: bfloat16 [2, 768, 768], P(None, None, 'mp'), may hold values from -0.375 to 0.375
- w_out: bfloat16 [768, 768], P('mp'), may hold values from -0.875 to 0.875
- b_out: float32 [768], replicated, may hold values from -3 to 3
- gain_one: float32 [768], replicated, may hold values from 0.5 to 1.5
- shift_one: float32 [768], replicated, may hold values from -3 to 3
- w_in: bfloat16 [768, 3072], P(None, 'mp'), may hold values from -0.21875 to 0.21875
- b_in: float32 [3072], P('mp'), may hold values from -3 to 3
- w_back: bfloat16 [3072, 768], P('mp'), may hold values from -0.109375 to 0.109375
- b_back: float32 [768], replicated, may hold values from -3 to 3
- gain_two: float32 [768], replicated, may hold values from 0.5 to 1.5
- shift_two: float32 [768], replicated, may hold values from -3 to 3
- cotangent: bfloat16 [16, 512, 768], P('dp'), may hold values from -6 to 6
Outputs:
- layer_out: bfloat16 [16, 512, 768], P('dp')
- grad_tokens: float32 [16, 512, 768], P('dp')
- grad_w_qkv: float32 [3, 768, 768], P(None, None, 'mp')
- grad_w_pos: float32 [2, 768, 768], P(None, None, 'mp')
- grad_w_out: float32 [768, 768], P('mp')
- grad_b_out: float32 [768], replicated
- grad_gain_one: float32 [768], replicated
- grad_shift_one: float32 [768], replicated
- grad_w_in: float32 [768, 3072], P(None, 'mp')
- grad_b_in: float32 [3072], P('mp')
- grad_w_back: float32 [3072, 768], P('mp')
- grad_b_back: float32 [768], replicated
- grad_gain_two: float32 [768], replicated
- grad_shift_two: float32 [768], replicated
Inputs may be any that keep to these rules, and one draw needn't show every extreme that they name: `lengths`: in every draw some page has all 512 tokens real.
All inputs are finite; a program needn't handle non-finite values.
Results may differ from a plain program's by a relative error of at most 0.015.
Values sent between devices are 32-bit elements; how exact they have to be, the bound alone decides.
No kernel may reach another device: no remote copies, remote signals or barrier semaphores. Data moves between devices by JAX's collectives and lax.ppermute only.
A program may use at most 128 MiB of HBM per device.

v0:
```python
from functools import partial
import math
import jax
import jax.numpy as jnp
from jax import lax
from jax.sharding import PartitionSpec as P

HEAD_DIM = 64


def sinusoid(coords, model_width):
    quarter = model_width // 4
    frequency = jnp.exp(jnp.arange(quarter, dtype=jnp.float32) * (-math.log(10000.0) / quarter))
    position = coords.astype(jnp.float32)
    phases = position[:, :, None] * frequency
    sin_cos = jnp.concatenate([jnp.sin(phases), jnp.cos(phases)], axis=2)
    return jnp.concatenate([sin_cos[0], sin_cos[1]], axis=1)


def layer_norm(values, norm_gain, norm_shift):
    center = values - jnp.mean(values, axis=-1, keepdims=True)
    spread = jnp.mean(center * center, axis=-1, keepdims=True)
    return center * lax.rsqrt(spread + 1e-05) * norm_gain + norm_shift


def exact_gelu(values):
    return jax.nn.gelu(values, approximate=False)


def page_scores(queries, key_rows, pos_query, pos_key, page_length):
    factor = 1.0 / math.sqrt(3.0 * queries.shape[2])
    scores = jnp.einsum("ihd,jhd->hij", queries, key_rows, preferred_element_type=jnp.float32)
    scores = scores + jnp.einsum(
        "ihd,jhd->hij", queries, pos_key, preferred_element_type=jnp.float32
    )
    scores = scores + jnp.einsum(
        "ihd,jhd->hij", pos_query, key_rows, preferred_element_type=jnp.float32
    )
    scores = scores * factor
    visible = jnp.arange(queries.shape[0]) < page_length
    return jnp.where(visible[None, None, :], scores, -1e30)


def attend_page(inputs):
    queries, key_rows, value_rows, pos_query, pos_key, page_length = inputs
    scores = page_scores(queries, key_rows, pos_query, pos_key, page_length)
    highest = jnp.max(scores, axis=2, keepdims=True)
    totals = jnp.sum(jnp.exp(scores - highest), axis=2, keepdims=True)
    log_total = highest + jnp.log(totals)
    weights = jnp.exp(scores - log_total).astype(jnp.bfloat16)
    mixed = jnp.einsum("hij,jhd->ihd", weights, value_rows, preferred_element_type=jnp.float32)
    return (mixed.astype(jnp.bfloat16), log_total)


def page_backward(inputs):
    queries, key_rows, value_rows, pos_query, pos_key, page_length, log_total, d_mixed = inputs
    factor = 1.0 / math.sqrt(3.0 * queries.shape[2])
    scores = page_scores(queries, key_rows, pos_query, pos_key, page_length)
    probs = jnp.exp(scores - log_total)
    weights = probs.astype(jnp.bfloat16)
    d_values = jnp.einsum("hij,ihd->jhd", weights, d_mixed, preferred_element_type=jnp.float32)
    d_probs = jnp.einsum("ihd,jhd->hij", d_mixed, value_rows, preferred_element_type=jnp.float32)
    d_scores = (probs * (d_probs - jnp.sum(d_probs * probs, axis=2, keepdims=True))).astype(
        jnp.bfloat16
    )
    by_key = jnp.einsum("hij,jhd->ihd", d_scores, key_rows, preferred_element_type=jnp.float32)
    by_pos_key = jnp.einsum("hij,jhd->ihd", d_scores, pos_key, preferred_element_type=jnp.float32)
    by_query = jnp.einsum("hij,ihd->jhd", d_scores, queries, preferred_element_type=jnp.float32)
    by_pos_query = jnp.einsum(
        "hij,ihd->jhd", d_scores, pos_query, preferred_element_type=jnp.float32
    )
    d_queries = ((by_key + by_pos_key) * factor).astype(jnp.bfloat16)
    d_pos_query = (by_key * factor).astype(jnp.bfloat16)
    d_keys = ((by_query + by_pos_query) * factor).astype(jnp.bfloat16)
    d_pos_key = (by_query * factor).astype(jnp.bfloat16)
    return (d_queries, d_keys, d_values.astype(jnp.bfloat16), d_pos_query, d_pos_key)


def forward(
    token_rows,
    position,
    lengths,
    w_qkv,
    w_pos,
    w_out,
    b_out,
    gain_one,
    shift_one,
    w_in,
    b_in,
    w_back,
    b_back,
    gain_two,
    shift_two,
):
    page_count = lengths.shape[0]
    page_len = token_rows.shape[0] // page_count
    heads_here = w_qkv.shape[2] // HEAD_DIM

    def split_heads(values):
        return values.astype(jnp.bfloat16).reshape(page_count, page_len, heads_here, HEAD_DIM)

    queries = split_heads(jnp.dot(token_rows, w_qkv[0], preferred_element_type=jnp.float32))
    key_rows = split_heads(jnp.dot(token_rows, w_qkv[1], preferred_element_type=jnp.float32))
    value_rows = split_heads(jnp.dot(token_rows, w_qkv[2], preferred_element_type=jnp.float32))
    pos_query = split_heads(jnp.dot(position, w_pos[0], preferred_element_type=jnp.float32))
    pos_key = split_heads(jnp.dot(position, w_pos[1], preferred_element_type=jnp.float32))
    mixed, log_total = lax.map(
        attend_page, (queries, key_rows, value_rows, pos_query, pos_key, lengths)
    )
    mixed = mixed.reshape(page_count * page_len, heads_here * HEAD_DIM)
    branch = lax.psum(jnp.dot(mixed, w_out, preferred_element_type=jnp.float32), "mp") + b_out
    first = token_rows.astype(jnp.float32) + branch
    normed = layer_norm(first, gain_one, shift_one)
    normed_low = normed.astype(jnp.bfloat16)
    hidden_pre = jnp.dot(normed_low, w_in, preferred_element_type=jnp.float32) + b_in
    hidden = exact_gelu(hidden_pre).astype(jnp.bfloat16)
    feed = lax.psum(jnp.dot(hidden, w_back, preferred_element_type=jnp.float32), "mp") + b_back
    second = normed + feed
    output = layer_norm(second, gain_two, shift_two)
    saved = (
        queries,
        key_rows,
        value_rows,
        pos_query,
        pos_key,
        mixed,
        log_total,
        first,
        normed,
        normed_low,
        hidden_pre,
        hidden,
        second,
    )
    return (output, saved)


def body(
    tokens,
    lengths,
    coords,
    w_qkv,
    w_pos,
    w_out,
    b_out,
    gain_one,
    shift_one,
    w_in,
    b_in,
    w_back,
    b_back,
    gain_two,
    shift_two,
    cotangent,
):
    page_count, page_len, model_width = tokens.shape
    token_rows = tokens.reshape(page_count * page_len, model_width)
    position = jax.vmap(partial(sinusoid, model_width=model_width))(coords)
    position = position.astype(jnp.bfloat16).reshape(page_count * page_len, model_width)
    weights_all = (
        w_qkv,
        w_pos,
        w_out,
        b_out,
        gain_one,
        shift_one,
        w_in,
        b_in,
        w_back,
        b_back,
        gain_two,
        shift_two,
    )
    output, saved = forward(token_rows, position, lengths, *weights_all)
    (
        queries,
        key_rows,
        value_rows,
        pos_query,
        pos_key,
        mixed,
        log_total,
        first,
        normed,
        normed_low,
        hidden_pre,
        hidden,
        second,
    ) = saved
    heads_here = w_qkv.shape[2] // HEAD_DIM
    d_output = cotangent.reshape(page_count * page_len, model_width).astype(jnp.float32)
    unused_two, pull_two = jax.vjp(layer_norm, second, gain_two, shift_two)
    d_second, d_gain_two, d_shift_two = pull_two(d_output)
    d_feed = d_second.astype(jnp.bfloat16)
    d_b_back = jnp.sum(d_feed.astype(jnp.float32), axis=0)
    d_w_back = jnp.dot(hidden.T, d_feed, preferred_element_type=jnp.float32)
    d_hidden = jnp.dot(d_feed, w_back.T, preferred_element_type=jnp.float32)
    unused_gelu, pull_gelu = jax.vjp(exact_gelu, hidden_pre)
    d_pre = pull_gelu(d_hidden)[0].astype(jnp.bfloat16)
    d_b_in = jnp.sum(d_pre.astype(jnp.float32), axis=0)
    d_w_in = jnp.dot(normed_low.T, d_pre, preferred_element_type=jnp.float32)
    ffn_terms = (d_w_in, d_b_in, d_w_back, d_b_back, d_gain_two, d_shift_two)
    d_normed = d_second + lax.psum(jnp.dot(d_pre, w_in.T, preferred_element_type=jnp.float32), "mp")
    unused_one, pull_one = jax.vjp(layer_norm, first, gain_one, shift_one)
    d_first, d_gain_one, d_shift_one = pull_one(d_normed)
    d_branch = d_first.astype(jnp.bfloat16)
    d_b_out = jnp.sum(d_branch.astype(jnp.float32), axis=0)
    d_w_out = jnp.dot(mixed.T, d_branch, preferred_element_type=jnp.float32)
    d_mixed = jnp.dot(d_branch, w_out.T, preferred_element_type=jnp.float32).astype(jnp.bfloat16)
    d_mixed = d_mixed.reshape(page_count, page_len, heads_here, HEAD_DIM)
    head_grads = lax.map(
        page_backward,
        (queries, key_rows, value_rows, pos_query, pos_key, lengths, log_total, d_mixed),
    )
    flat_grads = [
        piece.reshape(page_count * page_len, heads_here * HEAD_DIM) for piece in head_grads
    ]
    d_queries, d_keys, d_values, d_pos_query, d_pos_key = flat_grads
    d_w_qkv = jnp.stack(
        [
            jnp.dot(token_rows.T, d_queries, preferred_element_type=jnp.float32),
            jnp.dot(token_rows.T, d_keys, preferred_element_type=jnp.float32),
            jnp.dot(token_rows.T, d_values, preferred_element_type=jnp.float32),
        ]
    )
    d_w_pos = jnp.stack(
        [
            jnp.dot(position.T, d_pos_query, preferred_element_type=jnp.float32),
            jnp.dot(position.T, d_pos_key, preferred_element_type=jnp.float32),
        ]
    )
    input_part = jnp.dot(d_queries, w_qkv[0].T, preferred_element_type=jnp.float32)
    input_part = input_part + jnp.dot(d_keys, w_qkv[1].T, preferred_element_type=jnp.float32)
    input_part = input_part + jnp.dot(d_values, w_qkv[2].T, preferred_element_type=jnp.float32)
    d_tokens = d_first + lax.psum(input_part, "mp")
    summed = lax.psum(
        (
            d_w_qkv,
            d_w_pos,
            d_w_out,
            d_b_out,
            d_gain_one,
            d_shift_one,
            d_w_in,
            d_b_in,
            d_w_back,
            d_b_back,
            d_gain_two,
            d_shift_two,
        ),
        "dp",
    )
    attn_terms = summed[:6]
    ffn_terms = summed[6:]
    sum_w_qkv, sum_w_pos, sum_w_out, sum_b_out, sum_gain_one, sum_shift_one = attn_terms
    sum_w_in, sum_b_in, sum_w_back, sum_b_back, sum_gain_two, sum_shift_two = ffn_terms
    layer_out = output.astype(jnp.bfloat16).reshape(page_count, page_len, model_width)
    grad_tokens = d_tokens.reshape(page_count, page_len, model_width)
    return (
        layer_out,
        grad_tokens,
        sum_w_qkv,
        sum_w_pos,
        sum_w_out,
        sum_b_out,
        sum_gain_one,
        sum_shift_one,
        sum_w_in,
        sum_b_in,
        sum_w_back,
        sum_b_back,
        sum_gain_two,
        sum_shift_two,
    )


def solution(mesh):
    placed = (
        P("dp", None, None),
        P("dp"),
        P("dp", None, None),
        P(None, None, "mp"),
        P(None, None, "mp"),
        P("mp", None),
        P(),
        P(),
        P(),
        P(None, "mp"),
        P("mp"),
        P("mp", None),
        P(),
        P(),
        P(),
        P("dp", None, None),
    )
    return jax.shard_map(
        body,
        mesh=mesh,
        in_specs=placed,
        out_specs=(
            P("dp", None, None),
            P("dp", None, None),
            P(None, None, "mp"),
            P(None, None, "mp"),
            P("mp", None),
            P(),
            P(),
            P(),
            P(None, "mp"),
            P("mp"),
            P("mp", None),
            P(),
            P(),
            P(),
        ),
        check_vma=False,
    )
```

profile of v0, /device:TPU:0, one launch (start us, length us, event | category | flops | bytes accessed | tf_op | source)
XLA Modules:
  0.0 760.1 jit_solution(17825696523205868860)
XLA Ops:
  7.8 2.9 convolution_convert_fusion.3
  10.7 2.1 convolution_convert_fusion.4
  12.9 1.6 convolution_convert_fusion.5
  14.5 8.2 %multiply_sine_fusion = (bf16[2,2,512,192]{3,2,1,0:T(8,128)(2,1)S(1)}, bf16[2,2,512,192]{3,2,1,0:T(8,128)(2,1)S(1)}) fusion(f32[192]{0:T(256)S(1)} %copy-done.47, f32[2,2,512]{2,1,0:T(2,128)S(1)} %convert_element_type.111), kind=kLoop, calls=%fused_computation.137 | loop fusion | flops 1179648 | bytes 1581824 | tf_op jit(solution)/shard_map/vmap()/sin | solution.py:16
  23.8 1.4 convolution_convert_fusion.1
  25.3 1.4 convolution_convert_fusion.2
  27.7 1.3 reshape.196
  29.0 1.3 reshape.195
  30.4 10.8 %while.30 = (s32[]{:T(128)}, bf16[2,512,3,64]{1,3,2,0:T(8,128)(2,1)S(1)}, f32[2,3,512,1]{2,1,3,0:T(4,128)S(1)}, bf16[2,512,3,64]{1,3,2,0:T(8,128)(2,1)S(1)}, s32...) while((s32[]{:T(128)}, ...), condition=%wide.region_3.4_spmd, body=%wide.region_0.3_spmd.sunk | while | flops 409828352 | bytes 23657600 | solution.py:108
  41.7 3.3 fusion.129
  45.5 123.4 %all-reduce.8.cloned.1.call-done = f32[1024,768]{1,0:T(8,128)} async-done(((f32[1024,768]{1,0:T(8,128)}), f32[1024,768]{1,0:T(8,128)}) %all-reduce.8.cloned.1.call-update) | async-done | bytes 3145744 | tf_op jit(solution)/shard_map/psum | solution.py:112
  168.9 2.8 fusion.123
  173.3 9.6 %multiply_convert_fusion.3 = (bf16[1024,768]{1,0:T(8,128)(2,1)S(1)}, f32[1024,768]{1,0:T(8,128)}, f32[1024,768]{1,0:T(8,128)}) fusion(f32[768]{0:T(1024)S(1)} %copy-done.51, bf16[768,768]{1,0:T(8,128)(2,1)S(1)} %copy-done, f32[1024,768]{1,0:T(8,128)S(1)} %get-tuple-element.272, f32[768]{0:T(1024)S(1)} %copy-done.44, f32[768]{0:T(1024)S(1)} %copy-done.32, ...), kind=kOutput, calls=%fused_computation.119 | convolution fusion | flops 1263796224 | bytes 12207104 | tf_op jit(solution)/shard_map/dot_general | solution.py:116
  184.1 3.1 fusion.130
  187.3 120.2 %all-reduce.10.cloned.1.call-done = f32[1024,768]{1,0:T(8,128)} async-done(((f32[1024,768]{1,0:T(8,128)}), f32[1024,768]{1,0:T(8,128)}) %all-reduce.10.cloned.1.call-update) | async-done | bytes 3145744 | tf_op jit(solution)/shard_map/psum | solution.py:118
  307.5 3.9 fusion.121
  312.7 1.8 fusion.92
  314.5 2.6 fusion.120
  317.2 1.7 copy-done.5
  320.5 2.8 convert_reduce_fusion.2
  324.5 3.1 fusion.131
  327.9 120.0 %all-reduce.12.cloned.1.call-done = f32[1024,768]{1,0:T(8,128)} async-done(((f32[1024,768]{1,0:T(8,128)}), f32[1024,768]{1,0:T(8,128)}) %all-reduce.12.cloned.1.call-update) | async-done | bytes 3145744 | tf_op jit(solution)/shard_map/psum | solution.py:204
  447.9 5.2 multiply_reduce_fusion.1
  453.1 2.8 fusion.119
  456.0 1.6 copy-done.4
  463.9 22.3 %while.31 = (s32[]{:T(128)}, bf16[2,512,3,64]{1,3,2,0:T(8,128)(2,1)}, bf16[2,512,3,64]{1,3,2,0:T(8,128)(2,1)}, bf16[2,512,3,64]{1,3,2,0:T(8,128)(2,1)}, bf16[2,5...) while((s32[]{:T(128)}, ...), condition=%wide.region_17.18_spmd, body=%wide.region_15.17_spmd.sunk | while | flops 915700736 | bytes 53913936 | solution.py:212
  463.9 1.3 dynamic_slice.183
  467.9 1.3 subtract_exponential_fusion.2
  469.1 1.3 fusion.227
  475.0 1.3 dynamic_slice.183
  479.0 1.3 subtract_exponential_fusion.2
  480.2 1.3 fusion.227
  486.2 1.5 copy.65
  487.7 1.4 copy.66
  489.1 1.4 copy.67
  491.9 2.3 add_add_fusion.2
  494.5 4.9 fusion.133
  499.4 3.3 fusion.126
  507.6 1.3 pad_maximum_fusion
  508.9 1.3 fusion.132
  510.3 1.3 copy-done.9
  512.0 26.2 %all-reduce = (f32[768]{0:T(1024)}, f32[768]{0:T(1024)}, f32[768]{0:T(1024)}, f32[768]{0:T(1024)}, f32[768]{0:T(1024)}, /*index=5*/f32[768]{0:T(1024)}, f32[768]{0:T(1024)}) all-reduce(f32[768]{0:T(1024)S(1)} %copy-done.38, f32[768]{0:T(1024)S(1)} %copy-done.35, f32[768]{0:T(1024)S(1)} %copy-done.36, ...), channel_id=1, replica_groups=mesh['dp'=8,'mp'=4] {'dp'}, use_global_device_ids=true, to_apply=%region_23.24 | all-reduce | flops 5376 | bytes 43008 | tf_op jit(solution)/shard_map/psum | solution.py:237
  538.2 76.3 %all-reduce.14.cloned.1.call-done = f32[1024,768]{1,0:T(8,128)} async-done(((f32[1024,768]{1,0:T(8,128)}), f32[1024,768]{1,0:T(8,128)}) %all-reduce.14.cloned.1.call-update) | async-done | bytes 3145744 | tf_op jit(solution)/shard_map/psum | solution.py:236
  614.5 4.9 add_add_fusion.5
  619.3 126.4 %all-reduce.16.cloned.1.call-done = (f32[3,768,192]{1,2,0:T(8,128)}, f32[2,768,192]{1,2,0:T(8,128)}, f32[192,768]{1,0:T(8,128)}, f32[768,768]{1,0:T(8,128)}, f32[768,768]{1,0:T(8,128)}) async-done(((f32[3,768,192]{1,2,0:T(8,128)}, f32[2,768,192]{1,2,0:T(8,128)}, f32[192,768]{1,0:T(8,128)}, f32[768,768]{1,0:T(8,128)}, f32[768,768]{1,0:T(8,128)}), (f32[3,768,192]{1,2,0:T(8,128)}, f32[2,768,192]{1,2,0:T(8,128)}, ...) | async-done | bytes 8257552 | tf_op jit(solution)/shard_map/psum | solution.py:237
  745.7 2.9 copy.127
  750.5 1.4 copy.130
  751.9 1.4 copy.131
  (225 shorter events, 50.8 us)
Async XLA Ops:
  7.2 166.1 %copy-start = (bf16[768,768]{1,0:T(8,128)(2,1)S(1)}, bf16[768,768]{1,0:T(8,128)(2,1)}, u32[]{:S(2)}) copy-start(bf16[768,768]{1,0:T(8,128)(2,1)} %param.29) | copy-start | bytes 3538948
  7.2 5.7 copy-start.6
  7.2 161.7 %all-reduce.8.cloned.1.call-start = ((), (), s32[]{:S(2)}) async-start(), calls=%async_computation | async-start | bytes 6291456 | tf_op jit(solution)/shard_map/psum | solution.py:112
  7.8 6.7 copy-start.41
  7.8 6.7 copy-start.47
  23.5 1.7 copy-start.24
  23.5 1.7 copy-start.26
  23.8 2.8 copy-start.29
  41.2 3.8 copy-start.31
  45.0 262.5 %all-reduce.10.cloned.1.call-start = ((), (), s32[]{:S(2)}) async-start(), calls=%async_computation.1 | async-start | bytes 6291456 | tf_op jit(solution)/shard_map/psum | solution.py:118
  171.7 11.2 %copy-start.2 = (f32[1024,768]{1,0:T(8,128)}, f32[1024,768]{1,0:T(8,128)S(1)}, u32[]{:S(2)}) copy-start(f32[1024,768]{1,0:T(8,128)S(1)} %get-tuple-element.272) | copy-start | bytes 9437188
  171.7 1.5 copy-start.32
  171.8 1.5 copy-start.44
  173.3 10.8 %copy-start.48 = (bf16[768,768]{1,0:T(8,128)(2,1)S(1)}, bf16[768,768]{1,0:T(8,128)(2,1)}, u32[]{:S(2)}) copy-start(bf16[768,768]{1,0:T(8,128)(2,1)} %param.31) | copy-start | bytes 3538948
  187.2 120.3 %copy-start.42 = (f32[768]{0:T(1024)S(1)}, f32[768]{0:T(1024)}, u32[]{:S(2)}) copy-start(f32[768]{0:T(1024)} %param.32) | copy-start | bytes 9220
  187.2 260.7 %all-reduce.12.cloned.1.call-start = ((), (), s32[]{:S(2)}) async-start(), calls=%async_computation.2 | async-start | bytes 6291456 | tf_op jit(solution)/shard_map/psum | solution.py:204
  311.9 2.7 copy-start.43
  314.5 5.2 copy-start.57
  317.1 1.7 copy-start.5
  317.1 2.6 copy-start.49
  317.1 2.6 copy-start.52
  317.1 3.4 copy-start.56
  319.8 3.6 copy-start.21
  327.6 125.5 %copy-start.34 = (f32[1024]{0:T(1024)S(1)}, f32[1024]{0:T(1024)}, u32[]{:S(2)}) copy-start(f32[1024]{0:T(1024)} %copy-done.33) | copy-start | bytes 12292
  327.6 286.8 %all-reduce.14.cloned.1.call-start = ((), (), s32[]{:S(2)}) async-start(), calls=%async_computation.3 | async-start | bytes 6291456 | tf_op jit(solution)/shard_map/psum | solution.py:236
  456.0 1.7 copy-start.4
  456.0 3.8 copy-start.30
  471.9 1.6 copy-start.19
  483.0 1.6 copy-start.19
  486.2 4.5 copy-start.23
  494.2 5.2 copy-start.45
  494.2 251.5 %all-reduce.16.cloned.1.call-start = ((), (), s32[]{:S(2)}) async-start(), calls=%async_computation.4 | async-start | bytes 16515072 | tf_op jit(solution)/shard_map/psum | solution.py:237
  494.5 4.9 copy-start.3
  494.5 4.9 copy-start.55
  499.4 3.8 copy-start.16
  504.6 1.6 copy-start.7
  507.1 1.8 copy-start.11
  510.3 1.7 copy-start.35
  510.3 1.7 copy-start.36
  510.3 1.7 copy-start.37
  510.3 1.7 copy-start.38
  510.3 1.7 copy-start.40
  510.3 1.7 copy-start.46
  745.7 3.0 copy-start.22
  745.7 4.0 copy-start.28
  745.7 4.8 copy-start.13
  749.7 2.2 copy-start.12
  750.5 2.8 copy-start.1
  (21 other events, 23.8 us)
Sparse Core Ops, SparseCore 0:
  45.1 123.7 all-reduce.7
  187.3 120.0 all-reduce.9
  327.8 120.0 all-reduce.11
  494.3 120.0 all-reduce.13
  619.9 125.7 all-reduce.15
where the time goes:
time: 768 us; the launch traced here: 760 us
  waiting for transfers between devices  566 us (74%)
  matrix products  66.3 us (9%)
  other arithmetic  44.3 us (6%)
  local copies, waits for them, and re-layouts  40.9 us (5%)
  blocking collectives  26.2 us (3%)
  between operations  14.7 us (2%)
    psum x1, waiting for transfers between devices, body(): lax.psum((d_w_qkv, d_w_pos, d_w_out, d_b_out, d_gain_one, d_shift_one, d_...  126 us
    psum x1, waiting for transfers between devices, forward(): lax.psum(jnp.dot(mixed, w_out, preferred_element_type=jnp.float32), 'mp')  123 us
    psum x1, waiting for transfers between devices, forward(): lax.psum(jnp.dot(hidden, w_back, preferred_element_type=jnp.float32), 'mp')  120 us
    psum x1, waiting for transfers between devices, body(): lax.psum(jnp.dot(d_pre, w_in.T, preferred_element_type=jnp.float32), 'mp')  120 us
    psum x1, waiting for transfers between devices, body(): d_tokens = d_first + lax.psum(input_part, 'mp')  76.3 us
    psum x1, blocking collectives, body(): lax.psum((d_w_qkv, d_w_pos, d_w_out, d_b_out, d_gain_one, d_shift_one, d_...  26.2 us
    unnamed x115, local copies, waits for them, and re-layouts  19.5 us
  transfers between devices with their start and end apart: 5, of which 5 were waited for; matrix products, arithmetic and copies ran while one was open for 3% of the time, Pallas kernels for 0%

commit v1 on v0

--- a/solution.py
+++ b/solution.py
@@ -233,7 +233,7 @@
     input_part = jnp.dot(d_queries, w_qkv[0].T, preferred_element_type=jnp.float32)
     input_part = input_part + jnp.dot(d_keys, w_qkv[1].T, preferred_element_type=jnp.float32)
     input_part = input_part + jnp.dot(d_values, w_qkv[2].T, preferred_element_type=jnp.float32)
-    d_tokens = d_first + lax.psum(input_part, "mp")
+    d_tokens = d_first + jnp.sum(lax.all_gather(input_part, "mp"), axis=0)
     summed = lax.psum(
         (
             d_w_qkv,

time: 768 us -> 864 us (1.12)
  waiting for transfers between devices: 566 us -> 654 us
    all_gather x0 -> x1, waiting for transfers between devices: none -> 173 us  [body(): d_tokens = d_first + jnp.sum(lax.all_gather(input_part, 'mp'), axis=0)]
    psum x1 -> x0, waiting for transfers between devices: 76.3 us -> none  [body(): d_tokens = d_first + lax.psum(input_part, 'mp')]
    psum x1, waiting for transfers between devices: 126 us -> 117 us  [body(): lax.psum((d_w_qkv, d_w_pos, d_w_out, d_b_out, d_gain_one, d_shift_one, d_...]
where the time goes in v1:
time: 864 us; the launch traced here: 856 us
  waiting for transfers between devices  654 us (76%)
  matrix products  66.3 us (8%)
  other arithmetic  52.4 us (6%)
  local copies, waits for them, and re-layouts  41.1 us (5%)
  blocking collectives  26.2 us (3%)
  between operations  14.7 us (2%)
    all_gather x1, waiting for transfers between devices, body(): d_tokens = d_first + jnp.sum(lax.all_gather(input_part, 'mp'), axis=0)  173 us
    psum x1, waiting for transfers between devices, forward(): lax.psum(jnp.dot(mixed, w_out, preferred_element_type=jnp.float32), 'mp')  123 us
    psum x1, waiting for transfers between devices, forward(): lax.psum(jnp.dot(hidden, w_back, preferred_element_type=jnp.float32), 'mp')  120 us
    psum x1, waiting for transfers between devices, body(): lax.psum(jnp.dot(d_pre, w_in.T, preferred_element_type=jnp.float32), 'mp')  120 us
    psum x1, waiting for transfers between devices, body(): lax.psum((d_w_qkv, d_w_pos, d_w_out, d_b_out, d_gain_one, d_shift_one, d_...  117 us
    psum x1, blocking collectives, body(): lax.psum((d_w_qkv, d_w_pos, d_w_out, d_b_out, d_gain_one, d_shift_one, d_...  26.2 us
    unnamed x115, local copies, waits for them, and re-layouts  19.7 us
  transfers between devices with their start and end apart: 5, of which 5 were waited for; matrix products, arithmetic and copies ran while one was open for 3% of the time, Pallas kernels for 0%

profile of v1, /device:TPU:0, one launch (start us, length us, event | category | flops | bytes accessed | tf_op | source)
XLA Modules:
  0.0 856.2 jit_solution(14313444498328438055)
XLA Ops:
  7.8 2.9 convolution_convert_fusion.3
  10.7 2.1 convolution_convert_fusion.4
  12.9 1.6 convolution_convert_fusion.5
  14.5 8.2 multiply_sine_fusion
  23.8 1.4 convolution_convert_fusion.1
  25.3 1.4 convolution_convert_fusion.2
  27.7 1.3 reshape.196
  29.0 1.3 reshape.195
  30.4 10.8 %while.30 = (s32[]{:T(128)}, bf16[2,512,3,64]{1,3,2,0:T(8,128)(2,1)S(1)}, f32[2,3,512,1]{2,1,3,0:T(4,128)S(1)}, bf16[2,512,3,64]{1,3,2,0:T(8,128)(2,1)S(1)}, s32...) while((s32[]{:T(128)}, ...), condition=%wide.region_3.4_spmd, body=%wide.region_0.3_spmd.sunk | while | flops 409828352 | bytes 23657600 | solution.py:108
  41.7 3.3 fusion.129
  45.5 123.4 %all-reduce.7.cloned.1.call-done = f32[1024,768]{1,0:T(8,128)} async-done(((f32[1024,768]{1,0:T(8,128)}), f32[1024,768]{1,0:T(8,128)}) %all-reduce.7.cloned.1.call-update) | async-done | bytes 3145744 | tf_op jit(solution)/shard_map/psum | solution.py:112
  168.9 2.8 fusion.123
  173.3 9.6 %multiply_convert_fusion.3 = (bf16[1024,768]{1,0:T(8,128)(2,1)S(1)}, f32[1024,768]{1,0:T(8,128)}, f32[1024,768]{1,0:T(8,128)}) fusion(f32[768]{0:T(1024)S(1)} %copy-done.51, bf16[768,768]{1,0:T(8,128)(2,1)S(1)} %copy-done, f32[1024,768]{1,0:T(8,128)S(1)} %get-tuple-element.272, f32[768]{0:T(1024)S(1)} %copy-done.44, f32[768]{0:T(1024)S(1)} %copy-done.32, ...), kind=kOutput, calls=%fused_computation.119 | convolution fusion | flops 1263796224 | bytes 12207104 | tf_op jit(solution)/shard_map/dot_general | solution.py:116
  184.1 3.1 fusion.130
  187.3 120.2 %all-reduce.9.cloned.1.call-done = f32[1024,768]{1,0:T(8,128)} async-done(((f32[1024,768]{1,0:T(8,128)}), f32[1024,768]{1,0:T(8,128)}) %all-reduce.9.cloned.1.call-update) | async-done | bytes 3145744 | tf_op jit(solution)/shard_map/psum | solution.py:118
  307.5 3.9 fusion.121
  312.8 1.8 fusion.92
  314.6 2.6 fusion.120
  317.2 1.6 copy-done.5
  320.6 2.8 convert_reduce_fusion.2
  324.5 3.1 fusion.131
  327.9 120.0 %all-reduce.11.cloned.1.call-done = f32[1024,768]{1,0:T(8,128)} async-done(((f32[1024,768]{1,0:T(8,128)}), f32[1024,768]{1,0:T(8,128)}) %all-reduce.11.cloned.1.call-update) | async-done | bytes 3145744 | tf_op jit(solution)/shard_map/psum | solution.py:204
  447.9 5.2 multiply_reduce_fusion.1
  453.1 2.8 fusion.119
  456.0 1.6 copy-done.4
  463.9 22.1 %while.31 = (s32[]{:T(128)}, bf16[2,512,3,64]{1,3,2,0:T(8,128)(2,1)}, bf16[2,512,3,64]{1,3,2,0:T(8,128)(2,1)}, bf16[2,512,3,64]{1,3,2,0:T(8,128)(2,1)}, bf16[2,5...) while((s32[]{:T(128)}, ...), condition=%wide.region_17.18_spmd, body=%wide.region_15.17_spmd.sunk | while | flops 915700736 | bytes 53913936 | solution.py:212
  463.9 1.3 dynamic_slice.183
  467.8 1.3 subtract_exponential_fusion.2
  469.0 1.3 fusion.227
  474.9 1.3 dynamic_slice.183
  480.1 1.3 fusion.227
  486.0 1.5 copy.65
  487.5 1.4 copy.66
  489.0 1.4 copy.67
  491.7 2.3 add_add_fusion.2
  494.3 4.9 fusion.133
  499.2 3.3 fusion.126
  507.8 1.3 pad_maximum_fusion
  509.1 1.3 fusion.132
  510.5 1.3 copy-done.9
  512.1 26.2 %all-reduce = (f32[768]{0:T(1024)}, f32[768]{0:T(1024)}, f32[768]{0:T(1024)}, f32[768]{0:T(1024)}, f32[768]{0:T(1024)}, /*index=5*/f32[768]{0:T(1024)}, f32[768]{0:T(1024)}) all-reduce(f32[768]{0:T(1024)S(1)} %copy-done.38, f32[768]{0:T(1024)S(1)} %copy-done.35, f32[768]{0:T(1024)S(1)} %copy-done.36, ...), channel_id=1, replica_groups=mesh['dp'=8,'mp'=4] {'dp'}, use_global_device_ids=true, to_apply=%region_23.24 | all-reduce | flops 5376 | bytes 43008 | tf_op jit(solution)/shard_map/psum | solution.py:237
  538.3 173.1 %all-gather.3.cloned.1.call-done = f32[4096,768]{1,0:T(8,128)} async-done(((f32[1024,768]{1,0:T(8,128)}), f32[4096,768]{1,0:T(8,128)}) %all-gather.3.cloned.1.call-update) | async-done | bytes 12582928 | tf_op jit(solution)/shard_map/all_gather | solution.py:236
  711.4 7.5 reduce_sum.171
  718.9 5.6 add_add_fusion.5
  724.5 117.3 %all-reduce.13.cloned.1.call-done = (f32[3,768,192]{1,2,0:T(8,128)}, f32[2,768,192]{1,2,0:T(8,128)}, f32[192,768]{1,0:T(8,128)}, f32[768,768]{1,0:T(8,128)}, f32[768,768]{1,0:T(8,128)}) async-done(((f32[3,768,192]{1,2,0:T(8,128)}, f32[2,768,192]{1,2,0:T(8,128)}, f32[192,768]{1,0:T(8,128)}, f32[768,768]{1,0:T(8,128)}, f32[768,768]{1,0:T(8,128)}), (f32[3,768,192]{1,2,0:T(8,128)}, f32[2,768,192]{1,2,0:T(8,128)}, ...) | async-done | bytes 8257552 | tf_op jit(solution)/shard_map/psum | solution.py:237
  841.8 2.9 copy.126
  846.6 1.4 copy.129
  848.0 1.4 copy.130
  (226 shorter events, 52.4 us)
Async XLA Ops:
  7.2 166.1 %copy-start = (bf16[768,768]{1,0:T(8,128)(2,1)S(1)}, bf16[768,768]{1,0:T(8,128)(2,1)}, u32[]{:S(2)}) copy-start(bf16[768,768]{1,0:T(8,128)(2,1)} %param.29) | copy-start | bytes 3538948
  7.2 5.7 copy-start.6
  7.2 161.7 %all-reduce.7.cloned.1.call-start = ((), (), s32[]{:S(2)}) async-start(), calls=%async_computation | async-start | bytes 6291456 | tf_op jit(solution)/shard_map/psum | solution.py:112
  7.8 6.7 copy-start.41
  7.8 6.7 copy-start.47
  23.5 1.7 copy-start.24
  23.5 1.7 copy-start.26
  23.8 2.8 copy-start.29
  41.2 3.8 copy-start.31
  45.0 262.5 %all-reduce.9.cloned.1.call-start = ((), (), s32[]{:S(2)}) async-start(), calls=%async_computation.1 | async-start | bytes 6291456 | tf_op jit(solution)/shard_map/psum | solution.py:118
  171.7 11.2 %copy-start.2 = (f32[1024,768]{1,0:T(8,128)}, f32[1024,768]{1,0:T(8,128)S(1)}, u32[]{:S(2)}) copy-start(f32[1024,768]{1,0:T(8,128)S(1)} %get-tuple-element.272) | copy-start | bytes 9437188
  171.7 1.5 copy-start.32
  173.3 10.8 %copy-start.48 = (bf16[768,768]{1,0:T(8,128)(2,1)S(1)}, bf16[768,768]{1,0:T(8,128)(2,1)}, u32[]{:S(2)}) copy-start(bf16[768,768]{1,0:T(8,128)(2,1)} %param.31) | copy-start | bytes 3538948
  187.2 120.3 %copy-start.42 = (f32[768]{0:T(1024)S(1)}, f32[768]{0:T(1024)}, u32[]{:S(2)}) copy-start(f32[768]{0:T(1024)} %param.32) | copy-start | bytes 9220
  187.2 260.7 %all-reduce.11.cloned.1.call-start = ((), (), s32[]{:S(2)}) async-start(), calls=%async_computation.2 | async-start | bytes 6291456 | tf_op jit(solution)/shard_map/psum | solution.py:204
  311.9 2.7 copy-start.43
  314.6 5.2 copy-start.57
  317.2 1.7 copy-start.5
  317.2 2.6 copy-start.49
  317.2 2.6 copy-start.52
  317.2 3.4 copy-start.56
  319.8 3.6 copy-start.21
  327.7 125.5 %copy-start.34 = (f32[1024]{0:T(1024)S(1)}, f32[1024]{0:T(1024)}, u32[]{:S(2)}) copy-start(f32[1024]{0:T(1024)} %copy-done.33) | copy-start | bytes 12292
  327.7 383.7 %all-gather.3.cloned.1.call-start = ((), (), s32[]{:S(2)}) async-start(), calls=%async_computation.3 | async-start | bytes 15728640 | tf_op jit(solution)/shard_map/all_gather | solution.py:236
  456.0 1.6 copy-start.4
  456.0 3.7 copy-start.30
  471.8 1.6 copy-start.19
  482.9 1.6 copy-start.19
  486.0 4.5 copy-start.23
  494.0 5.2 copy-start.45
  494.0 347.8 %all-reduce.13.cloned.1.call-start = ((), (), s32[]{:S(2)}) async-start(), calls=%async_computation.4 | async-start | bytes 16515072 | tf_op jit(solution)/shard_map/psum | solution.py:237
  494.3 4.9 copy-start.3
  494.3 4.9 copy-start.55
  499.2 3.8 copy-start.16
  502.5 1.7 copy-start.27
  504.7 1.6 copy-start.7
  507.3 1.8 copy-start.11
  510.4 1.7 copy-start.35
  510.4 1.7 copy-start.36
  510.4 1.7 copy-start.37
  510.4 1.7 copy-start.38
  510.4 1.7 copy-start.40
  510.4 1.7 copy-start.46
  841.8 3.0 copy-start.22
  841.8 4.0 copy-start.28
  841.8 4.8 copy-start.13
  845.8 2.2 copy-start.12
  846.6 2.8 copy-start.1
  (21 other events, 24.1 us)
Sparse Core Ops, SparseCore 0:
  45.1 123.7 all-reduce.6
  187.4 120.0 all-reduce.8
  327.8 120.0 all-reduce.10
  494.2 217.2 all-gather.2
  716.9 124.9 all-reduce.12
